TPU v7x, 256 devices: a whole 4x4x8 slice. The times are simulated.
256 devices in a mesh: dp: 8 (over z), ctx: 32 (over x, y, core).
Axes of the slice: x: 4, y: 4, z: 8, core: 2. Of those that a mesh axis runs over, the one named last changes fastest.
Arguments:
- queries: bfloat16 [8, 4096, 4096], P('dp', 'ctx'), may hold values from -120 to 120
- layer_input: bfloat16 [8, 4096, 4096], P('dp', 'ctx'), may hold values from -6 to 6
- key_value_weight: bfloat16 [4096, 1024], P(('dp', 'ctx')), may hold values from -0.25 to 0.25
- output_gradient: bfloat16 [8, 4096, 4096], P('dp', 'ctx'), may hold values from -6 to 6
- document_lengths: int32 [8, 32], P('dp'), may hold values from 1 to 1024, 4096 in all within a row
Outputs:
- attended: bfloat16 [8, 4096, 4096], P('dp', 'ctx')
- query_grad: bfloat16 [8, 4096, 4096], P('dp', 'ctx')
- input_grad: bfloat16 [8, 4096, 4096], P('dp', 'ctx')
Inputs may be any that keep to these rules, and one draw needn't show every extreme that they name: `document_lengths`: each row holds the lengths of the 32 documents of one sequence in order; they sum to 4096, and one of them is exactly 1024.
All inputs are finite; a program needn't handle non-finite values.
Results may differ from a plain program's by a relative error of at most 0.02.
The roundings to bfloat16 on the way count: a program that leaves them out, or rounds other values in their place, can miss the bound.
Values may be sent and summed in bfloat16 or wider, within the bound.
A program may use at most 128 MiB of HBM per device.

v0:
```python
import math
import jax
import jax.numpy as jnp
from jax import lax
from jax.sharding import PartitionSpec as P

QUERY_HEADS = 32
KEY_VALUE_HEADS = 4
HEAD_SIZE = 128
masked_score = -1e30


def from_behind(value, axis, steps):
    count = lax.axis_size(axis)
    first, last = (max(0, -steps), min(count, count - steps))
    return lax.ppermute(value, axis, [(source, source + steps) for source in range(first, last)])


def document_of(positions, ends):
    return jnp.sum((positions[..., None] >= ends).astype(jnp.int32), axis=-1)


def attend(query_tile_block, gradient_block, key_blocks, query_start, key_starts, ends):
    row_indices = query_tile_block.shape[0]
    width = query_tile_block.shape[-1]
    heads = query_tile_block.shape[1]
    head_group = query_tile_block.shape[2]
    count = key_blocks.shape[1]
    scale = 1.0 / math.sqrt(width)
    query_start = jnp.asarray(query_start, jnp.int32)
    query_pos = query_start + jnp.arange(row_indices, dtype=jnp.int32)
    query_doc = document_of(query_pos, ends)
    first_doc = document_of(query_start, ends)
    last_query = query_start + row_indices - 1

    def mask_of(key_start):
        key_pos = key_start + jnp.arange(count, dtype=jnp.int32)
        key_doc = document_of(key_pos, ends)
        allowed = (
            (query_doc[:, None] == key_doc[None, :])
            & (key_pos[None, :] <= query_pos[:, None])
            & (key_pos[None, :] >= 0)
        )
        last_key = jnp.minimum(key_start + count - 1, last_query)
        live = (
            (key_start <= last_query)
            & (key_start + count - 1 >= 0)
            & (document_of(last_key, ends) >= first_doc)
        )
        return (allowed, live)

    def scores(block_slice):
        return scale * jnp.einsum(
            "qhgd,khd->hgqk",
            query_tile_block,
            block_slice[..., :width],
            preferred_element_type=jnp.float32,
        )

    def forward_step(state, item):
        block_slice, key_start = item
        allowed, live = mask_of(key_start)

        def forward(state):
            highest, total, accum = state
            score = scores(block_slice)
            newest = jnp.maximum(highest, jnp.max(jnp.where(allowed, score, masked_score), axis=-1))
            weight = jnp.exp(jnp.where(allowed, score - newest[..., None], masked_score))
            factor = jnp.exp(highest - newest)
            total = total * factor + jnp.sum(weight, axis=-1)
            mixed = jnp.einsum(
                "hgqk,khd->qhgd",
                weight.astype(jnp.bfloat16),
                block_slice[..., width:],
                preferred_element_type=jnp.float32,
            )
            accum = accum * jnp.transpose(factor, (2, 0, 1))[..., None] + mixed
            return (newest, total, accum)

        return (lax.cond(live, forward, lambda kept: kept, state), None)

    state = (
        jnp.full((heads, head_group, row_indices), masked_score, jnp.float32),
        jnp.zeros((heads, head_group, row_indices), jnp.float32),
        jnp.zeros(query_tile_block.shape, jnp.float32),
    )
    state, unused = lax.scan(forward_step, state, (key_blocks, key_starts))
    highest, total, accum = state
    output = (accum / jnp.transpose(total, (2, 0, 1))[..., None]).astype(jnp.bfloat16)
    logsum = highest + jnp.log(total)
    product = jnp.transpose(
        jnp.sum(gradient_block.astype(jnp.float32) * output.astype(jnp.float32), axis=-1), (1, 2, 0)
    )

    def backward_step(query_sum, item):
        block_slice, key_start = item
        allowed, live = mask_of(key_start)

        def backward(query_sum):
            score = scores(block_slice)
            prob = jnp.exp(jnp.where(allowed, score - logsum[..., None], masked_score))
            pressure = jnp.einsum(
                "qhgd,khd->hgqk",
                gradient_block,
                block_slice[..., width:],
                preferred_element_type=jnp.float32,
            )
            slope = (prob * (pressure - product[..., None])).astype(jnp.bfloat16)
            query_sum = query_sum + jnp.einsum(
                "hgqk,khd->qhgd",
                slope,
                block_slice[..., :width],
                preferred_element_type=jnp.float32,
            )
            key_part = scale * jnp.einsum(
                "hgqk,qhgd->khd", slope, query_tile_block, preferred_element_type=jnp.float32
            )
            value_part = jnp.einsum(
                "hgqk,qhgd->khd",
                prob.astype(jnp.bfloat16),
                gradient_block,
                preferred_element_type=jnp.float32,
            )
            return (query_sum, jnp.concatenate([key_part, value_part], axis=-1))

        def skipped(query_sum):
            return (query_sum, jnp.zeros(block_slice.shape, jnp.float32))

        return lax.cond(live, backward, skipped, query_sum)

    query_sum, pieces = lax.scan(
        backward_step, jnp.zeros(query_tile_block.shape, jnp.float32), (key_blocks, key_starts)
    )
    return (output, (scale * query_sum).astype(jnp.bfloat16), pieces)


def shards(queries, layer_input, key_value_weight, output_gradient, document_lengths):
    inputs = layer_input[0]
    row_indices = inputs.shape[0]
    ends = jnp.cumsum(document_lengths[0])
    columns_all = key_value_weight.shape[1]
    half_length = columns_all // 2
    projected_input = jnp.dot(
        inputs,
        lax.all_gather(key_value_weight, ("dp", "ctx"), axis=0, tiled=True),
        preferred_element_type=jnp.float32,
    )
    projected_input = projected_input.astype(jnp.bfloat16)
    key_rows = projected_input[:, :half_length].reshape(row_indices, KEY_VALUE_HEADS, HEAD_SIZE)
    value_rows = projected_input[:, half_length:].reshape(row_indices, KEY_VALUE_HEADS, HEAD_SIZE)
    paired = jnp.concatenate([key_rows, value_rows], axis=-1)
    devices = lax.axis_size("ctx")
    window_reach = devices // 4
    head_group = QUERY_HEADS // KEY_VALUE_HEADS
    offsets = jnp.arange(window_reach + 1, dtype=jnp.int32) * row_indices
    query_tile_block = queries[0].reshape(row_indices, KEY_VALUE_HEADS, head_group, HEAD_SIZE)
    gradient_block = output_gradient[0].reshape(row_indices, KEY_VALUE_HEADS, head_group, HEAD_SIZE)
    start = lax.axis_index("ctx") * row_indices
    blocks = [paired]
    for offset in range(window_reach):
        blocks.append(from_behind(blocks[-1], "ctx", 1))
    stacked = jnp.stack(blocks)
    output, query_sum, pieces = attend(
        query_tile_block, gradient_block, stacked, start, start - offsets, ends
    )
    carried = pieces[window_reach]
    for offset in range(window_reach - 1, -1, -1):
        carried = from_behind(carried, "ctx", -1) + pieces[offset]
    attended = output.reshape(row_indices, QUERY_HEADS * HEAD_SIZE)
    query_grad = query_sum.reshape(row_indices, QUERY_HEADS * HEAD_SIZE)
    gradient_value = carried.astype(jnp.bfloat16)
    flat = jnp.concatenate(
        [
            gradient_value[..., :HEAD_SIZE].reshape(row_indices, KEY_VALUE_HEADS * HEAD_SIZE),
            gradient_value[..., HEAD_SIZE:].reshape(row_indices, KEY_VALUE_HEADS * HEAD_SIZE),
        ],
        axis=1,
    )
    input_grad = lax.dot_general(
        flat,
        lax.all_gather(key_value_weight, ("dp", "ctx"), axis=0, tiled=True),
        (((1,), (1,)), ((), ())),
        preferred_element_type=jnp.float32,
    )
    return (attended[None], query_grad[None], input_grad.astype(jnp.bfloat16)[None])


def solution(mesh):
    return jax.shard_map(
        shards,
        mesh=mesh,
        in_specs=(
            P("dp", "ctx", None),
            P("dp", "ctx", None),
            P(("dp", "ctx"), None),
            P("dp", "ctx", None),
            P("dp", None),
        ),
        out_specs=(P("dp", "ctx", None), P("dp", "ctx", None), P("dp", "ctx", None)),
        check_vma=False,
    )
```

profile of v0, /device:TPU:57, one launch (start us, length us, event | category | flops | bytes accessed | tf_op | source)
XLA Modules:
  0.0 591.8 jit_solution(6829735065192717386)
XLA Ops:
  7.9 123.9 %all-gather.2.cloned.1.call-done = bf16[4096,1024]{1,0:T(8,128)(2,1)} async-done(((bf16[16,1024]{1,0:T(8,128)(2,1)}), bf16[4096,1024]{1,0:T(8,128)(2,1)}) %all-gather.2.cloned.1.call-update) | async-done | bytes 8388624 | tf_op jit(solution)/shard_map/all_gather | solution.py:145
  131.9 4.6 convolution_convert_fusion.1
  136.6 2.9 collective-permute-start
  139.5 3.3 collective-permute-done
  142.8 6.5 %collective-permute-start.1 = (bf16[128,4,256]{2,0,1:T(8,128)(2,1)S(1)}, bf16[128,4,256]{2,0,1:T(8,128)(2,1)S(1)}, u32[]{:S(2)}, u32[]{:S(2)}) collective-permute-start(bf16[128,4,256]{2,0,1:T(8,128)(2,1)S(1)} %collective-permute-done), channel_id=1, source_target_pairs={{0,1},{1,2},{2,3},{3,4},{4,5},{5,6},{6,7},{7,8},{8,9},{9,10},{10,1... | collective-permute-start | bytes 786440 | tf_op jit(solution)/shard_map/ppermute | solution.py:16
  149.3 3.3 collective-permute-done.1
  152.6 6.5 %collective-permute-start.2 = (bf16[128,4,256]{2,0,1:T(8,128)(2,1)S(1)}, bf16[128,4,256]{2,0,1:T(8,128)(2,1)}, u32[]{:S(2)}, u32[]{:S(2)}) collective-permute-start(bf16[128,4,256]{2,0,1:T(8,128)(2,1)S(1)} %collective-permute-done.1), channel_id=1, source_target_pairs={{0,1},{1,2},{2,3},{3,4},{4,5},{5,6},{6,7},{7,8},{8,9},{9,10},{10,1... | collective-permute-start | bytes 786440 | tf_op jit(solution)/shard_map/ppermute | solution.py:16
  159.1 3.3 collective-permute-done.2
  162.4 6.6 %collective-permute-start.3 = (bf16[128,4,256]{2,0,1:T(8,128)(2,1)}, bf16[128,4,256]{2,0,1:T(8,128)(2,1)}, u32[]{:S(2)}, u32[]{:S(2)}) collective-permute-start(bf16[128,4,256]{2,0,1:T(8,128)(2,1)} %collective-permute-done.2), channel_id=1, source_target_pairs={{0,1},{1,2},{2,3},{3,4},{4,5},{5,6},{6,7},{7,8},{8,9},{9,10},{10,1... | collective-permute-start | bytes 786440 | tf_op jit(solution)/shard_map/ppermute | solution.py:16
  173.6 5.5 collective-permute-start.4
  182.7 6.4 %collective-permute-start.5 = (bf16[128,4,256]{2,0,1:T(8,128)(2,1)S(1)}, bf16[128,4,256]{2,0,1:T(8,128)(2,1)S(1)}, u32[]{:S(2)}, u32[]{:S(2)}) collective-permute-start(bf16[128,4,256]{2,0,1:T(8,128)(2,1)S(1)} %collective-permute-done.4), channel_id=1, source_target_pairs={{0,1},{1,2},{2,3},{3,4},{4,5},{5,6},{6,7},{7,8},{8,9},{9,10},{10,1... | collective-permute-start | bytes 786440 | tf_op jit(solution)/shard_map/ppermute | solution.py:16
  192.4 6.4 %collective-permute-start.6 = (bf16[128,4,256]{2,0,1:T(8,128)(2,1)S(1)}, bf16[128,4,256]{2,0,1:T(8,128)(2,1)S(1)}, u32[]{:S(2)}, u32[]{:S(2)}) collective-permute-start(bf16[128,4,256]{2,0,1:T(8,128)(2,1)S(1)} %collective-permute-done.5), channel_id=1, source_target_pairs={{0,1},{1,2},{2,3},{3,4},{4,5},{5,6},{6,7},{7,8},{8,9},{9,10},{10,1... | collective-permute-start | bytes 786440 | tf_op jit(solution)/shard_map/ppermute | solution.py:16
  202.2 6.5 %collective-permute-start.7 = (bf16[128,4,256]{2,0,1:T(8,128)(2,1)S(1)}, bf16[128,4,256]{2,0,1:T(8,128)(2,1)S(1)}, u32[]{:S(2)}, u32[]{:S(2)}) collective-permute-start(bf16[128,4,256]{2,0,1:T(8,128)(2,1)S(1)} %collective-permute-done.6), channel_id=1, source_target_pairs={{0,1},{1,2},{2,3},{3,4},{4,5},{5,6},{6,7},{7,8},{8,9},{9,10},{10,1... | collective-permute-start | bytes 786440 | tf_op jit(solution)/shard_map/ppermute | solution.py:16
  214.2 101.9 %while.39 = (s32[]{:T(128)}, f32[4,8,128]{2,1,0:T(8,128)S(1)}, f32[4,8,128]{2,1,0:T(8,128)S(1)}, f32[128,4,8,128]{3,0,2,1:T(8,128)}, s32[9]{0:T(128)S(1)}, /*ind...) while((s32[]{:T(128)}, f32[4,8,128]{2,1,0:T(8,128)S(1)}, ...), condition=%wide.region_10.11_spmd.clone, body=%wide.region_3.10_spmd.clone.sunk | while | flops 275341920 | bytes 29466576 | solution.py:87
  218.8 7.6 %conditional.6 = ((f32[4,8,128]{2,1,0:T(8,128)S(1)}, f32[4,8,128]{2,1,0:T(8,128)S(1)}, f32[128,4,8,128]{3,0,2,1:T(8,128)})) conditional(s32[]{:T(128)} %convert_element_type.143, (f32[4,8,128]{2,1,0:T(8,128)S(1)}, f32[4,8,128]{2,1,0:T(8,128)S(1)}, f32[128,4,8,128]{3,0,2,1:T(8,128)}) %tuple.123, (s32[128]{0:T(128)S(1)}, s32[128,32]{1,0:T(8,128)S(1)}, ...), branch_computations={%region_5.5_spmd, %region_6.9_spmd} | conditional | flops 275333504 | bytes 29447532 | solution.py:80
  230.9 7.6 %conditional.6 = ((f32[4,8,128]{2,1,0:T(8,128)S(1)}, f32[4,8,128]{2,1,0:T(8,128)S(1)}, f32[128,4,8,128]{3,0,2,1:T(8,128)})) conditional(s32[]{:T(128)} %convert_element_type.143, (f32[4,8,128]{2,1,0:T(8,128)S(1)}, f32[4,8,128]{2,1,0:T(8,128)S(1)}, f32[128,4,8,128]{3,0,2,1:T(8,128)}) %tuple.123, (s32[128]{0:T(128)S(1)}, s32[128,32]{1,0:T(8,128)S(1)}, ...), branch_computations={%region_5.5_spmd, %region_6.9_spmd} | conditional | flops 275333504 | bytes 29447532 | solution.py:80
  233.5 1.8 fusion.4
  243.1 7.6 %conditional.6 = ((f32[4,8,128]{2,1,0:T(8,128)S(1)}, f32[4,8,128]{2,1,0:T(8,128)S(1)}, f32[128,4,8,128]{3,0,2,1:T(8,128)})) conditional(s32[]{:T(128)} %convert_element_type.143, (f32[4,8,128]{2,1,0:T(8,128)S(1)}, f32[4,8,128]{2,1,0:T(8,128)S(1)}, f32[128,4,8,128]{3,0,2,1:T(8,128)}) %tuple.123, (s32[128]{0:T(128)S(1)}, s32[128,32]{1,0:T(8,128)S(1)}, ...), branch_computations={%region_5.5_spmd, %region_6.9_spmd} | conditional | flops 275333504 | bytes 29447532 | solution.py:80
  245.7 1.8 fusion.4
  255.3 7.6 %conditional.6 = ((f32[4,8,128]{2,1,0:T(8,128)S(1)}, f32[4,8,128]{2,1,0:T(8,128)S(1)}, f32[128,4,8,128]{3,0,2,1:T(8,128)})) conditional(s32[]{:T(128)} %convert_element_type.143, (f32[4,8,128]{2,1,0:T(8,128)S(1)}, f32[4,8,128]{2,1,0:T(8,128)S(1)}, f32[128,4,8,128]{3,0,2,1:T(8,128)}) %tuple.123, (s32[128]{0:T(128)S(1)}, s32[128,32]{1,0:T(8,128)S(1)}, ...), branch_computations={%region_5.5_spmd, %region_6.9_spmd} | conditional | flops 275333504 | bytes 29447532 | solution.py:80
  267.5 7.6 %conditional.6 = ((f32[4,8,128]{2,1,0:T(8,128)S(1)}, f32[4,8,128]{2,1,0:T(8,128)S(1)}, f32[128,4,8,128]{3,0,2,1:T(8,128)})) conditional(s32[]{:T(128)} %convert_element_type.143, (f32[4,8,128]{2,1,0:T(8,128)S(1)}, f32[4,8,128]{2,1,0:T(8,128)S(1)}, f32[128,4,8,128]{3,0,2,1:T(8,128)}) %tuple.123, (s32[128]{0:T(128)S(1)}, s32[128,32]{1,0:T(8,128)S(1)}, ...), branch_computations={%region_5.5_spmd, %region_6.9_spmd} | conditional | flops 275333504 | bytes 29447532 | solution.py:80
  279.6 7.6 %conditional.6 = ((f32[4,8,128]{2,1,0:T(8,128)S(1)}, f32[4,8,128]{2,1,0:T(8,128)S(1)}, f32[128,4,8,128]{3,0,2,1:T(8,128)})) conditional(s32[]{:T(128)} %convert_element_type.143, (f32[4,8,128]{2,1,0:T(8,128)S(1)}, f32[4,8,128]{2,1,0:T(8,128)S(1)}, f32[128,4,8,128]{3,0,2,1:T(8,128)}) %tuple.123, (s32[128]{0:T(128)S(1)}, s32[128,32]{1,0:T(8,128)S(1)}, ...), branch_computations={%region_5.5_spmd, %region_6.9_spmd} | conditional | flops 275333504 | bytes 29447532 | solution.py:80
  282.2 1.8 fusion.4
  291.8 7.6 %conditional.6 = ((f32[4,8,128]{2,1,0:T(8,128)S(1)}, f32[4,8,128]{2,1,0:T(8,128)S(1)}, f32[128,4,8,128]{3,0,2,1:T(8,128)})) conditional(s32[]{:T(128)} %convert_element_type.143, (f32[4,8,128]{2,1,0:T(8,128)S(1)}, f32[4,8,128]{2,1,0:T(8,128)S(1)}, f32[128,4,8,128]{3,0,2,1:T(8,128)}) %tuple.123, (s32[128]{0:T(128)S(1)}, s32[128,32]{1,0:T(8,128)S(1)}, ...), branch_computations={%region_5.5_spmd, %region_6.9_spmd} | conditional | flops 275333504 | bytes 29447532 | solution.py:80
  304.0 7.6 %conditional.6 = ((f32[4,8,128]{2,1,0:T(8,128)S(1)}, f32[4,8,128]{2,1,0:T(8,128)S(1)}, f32[128,4,8,128]{3,0,2,1:T(8,128)})) conditional(s32[]{:T(128)} %convert_element_type.143, (f32[4,8,128]{2,1,0:T(8,128)S(1)}, f32[4,8,128]{2,1,0:T(8,128)S(1)}, f32[128,4,8,128]{3,0,2,1:T(8,128)}) %tuple.123, (s32[128]{0:T(128)S(1)}, s32[128,32]{1,0:T(8,128)S(1)}, ...), branch_computations={%region_5.5_spmd, %region_6.9_spmd} | conditional | flops 275333504 | bytes 29447532 | solution.py:80
  316.2 2.9 copy.49
  319.1 3.0 multiply_reduce_fusion
  323.7 125.9 %while.40 = (s32[]{:T(128)}, f32[128,4,8,128]{3,0,2,1:T(8,128)}, f32[9,128,4,256]{1,3,2,0:T(8,128)}, s32[9]{0:T(128)S(1)}, s32[]{:T(128)}, /*index=5*/s32[32]{0:...) while((s32[]{:T(128)}, f32[128,4,8,128]{3,0,2,1:T(8,128)}, ...), condition=%wide.region_17.18_spmd.clone, body=%wide.region_12.17_spmd.clone.sunk | while | flops 675558016 | bytes 38248896 | solution.py:131
  328.4 8.2 %conditional.7 = (f32[128,4,8,128]{3,0,2,1:T(8,128)}, f32[1,128,4,256]{1,3,2,0:T(8,128)}) conditional(s32[]{:T(128)} %convert_element_type.146, f32[128,4,8,128]{3,0,2,1:T(8,128)} %get-tuple-element.1136, (s32[128]{0:T(128)S(1)}, s32[128,32]{1,0:T(8,128)S(1)}, s32[]{:T(128)}, s32[1,128]{1,0:T(1,128)S(1)}, s32[]{:T(128)}, ...), branch_computations={%region_14.14_spmd, %region_15.16_spmd} | conditional | flops 675549568 | bytes 37180764 | solution.py:129
  336.6 1.9 constant_dynamic-update-slice_fusion.2
  343.3 8.2 %conditional.7 = (f32[128,4,8,128]{3,0,2,1:T(8,128)}, f32[1,128,4,256]{1,3,2,0:T(8,128)}) conditional(s32[]{:T(128)} %convert_element_type.146, f32[128,4,8,128]{3,0,2,1:T(8,128)} %get-tuple-element.1136, (s32[128]{0:T(128)S(1)}, s32[128,32]{1,0:T(8,128)S(1)}, s32[]{:T(128)}, s32[1,128]{1,0:T(1,128)S(1)}, s32[]{:T(128)}, ...), branch_computations={%region_14.14_spmd, %region_15.16_spmd} | conditional | flops 675549568 | bytes 37180764 | solution.py:129
  351.5 1.9 constant_dynamic-update-slice_fusion.2
  358.1 8.2 %conditional.7 = (f32[128,4,8,128]{3,0,2,1:T(8,128)}, f32[1,128,4,256]{1,3,2,0:T(8,128)}) conditional(s32[]{:T(128)} %convert_element_type.146, f32[128,4,8,128]{3,0,2,1:T(8,128)} %get-tuple-element.1136, (s32[128]{0:T(128)S(1)}, s32[128,32]{1,0:T(8,128)S(1)}, s32[]{:T(128)}, s32[1,128]{1,0:T(1,128)S(1)}, s32[]{:T(128)}, ...), branch_computations={%region_14.14_spmd, %region_15.16_spmd} | conditional | flops 675549568 | bytes 37180764 | solution.py:129
  366.3 1.9 constant_dynamic-update-slice_fusion.2
  372.9 8.2 %conditional.7 = (f32[128,4,8,128]{3,0,2,1:T(8,128)}, f32[1,128,4,256]{1,3,2,0:T(8,128)}) conditional(s32[]{:T(128)} %convert_element_type.146, f32[128,4,8,128]{3,0,2,1:T(8,128)} %get-tuple-element.1136, (s32[128]{0:T(128)S(1)}, s32[128,32]{1,0:T(8,128)S(1)}, s32[]{:T(128)}, s32[1,128]{1,0:T(1,128)S(1)}, s32[]{:T(128)}, ...), branch_computations={%region_14.14_spmd, %region_15.16_spmd} | conditional | flops 675549568 | bytes 37180764 | solution.py:129
  381.1 1.9 constant_dynamic-update-slice_fusion.2
  387.7 8.2 %conditional.7 = (f32[128,4,8,128]{3,0,2,1:T(8,128)}, f32[1,128,4,256]{1,3,2,0:T(8,128)}) conditional(s32[]{:T(128)} %convert_element_type.146, f32[128,4,8,128]{3,0,2,1:T(8,128)} %get-tuple-element.1136, (s32[128]{0:T(128)S(1)}, s32[128,32]{1,0:T(8,128)S(1)}, s32[]{:T(128)}, s32[1,128]{1,0:T(1,128)S(1)}, s32[]{:T(128)}, ...), branch_computations={%region_14.14_spmd, %region_15.16_spmd} | conditional | flops 675549568 | bytes 37180764 | solution.py:129
  395.9 1.9 constant_dynamic-update-slice_fusion.2
  402.5 8.2 %conditional.7 = (f32[128,4,8,128]{3,0,2,1:T(8,128)}, f32[1,128,4,256]{1,3,2,0:T(8,128)}) conditional(s32[]{:T(128)} %convert_element_type.146, f32[128,4,8,128]{3,0,2,1:T(8,128)} %get-tuple-element.1136, (s32[128]{0:T(128)S(1)}, s32[128,32]{1,0:T(8,128)S(1)}, s32[]{:T(128)}, s32[1,128]{1,0:T(1,128)S(1)}, s32[]{:T(128)}, ...), branch_computations={%region_14.14_spmd, %region_15.16_spmd} | conditional | flops 675549568 | bytes 37180764 | solution.py:129
  410.7 1.9 constant_dynamic-update-slice_fusion.2
  417.3 8.2 %conditional.7 = (f32[128,4,8,128]{3,0,2,1:T(8,128)}, f32[1,128,4,256]{1,3,2,0:T(8,128)}) conditional(s32[]{:T(128)} %convert_element_type.146, f32[128,4,8,128]{3,0,2,1:T(8,128)} %get-tuple-element.1136, (s32[128]{0:T(128)S(1)}, s32[128,32]{1,0:T(8,128)S(1)}, s32[]{:T(128)}, s32[1,128]{1,0:T(1,128)S(1)}, s32[]{:T(128)}, ...), branch_computations={%region_14.14_spmd, %region_15.16_spmd} | conditional | flops 675549568 | bytes 37180764 | solution.py:129
  425.5 1.9 constant_dynamic-update-slice_fusion.2
  432.1 8.2 %conditional.7 = (f32[128,4,8,128]{3,0,2,1:T(8,128)}, f32[1,128,4,256]{1,3,2,0:T(8,128)}) conditional(s32[]{:T(128)} %convert_element_type.146, f32[128,4,8,128]{3,0,2,1:T(8,128)} %get-tuple-element.1136, (s32[128]{0:T(128)S(1)}, s32[128,32]{1,0:T(8,128)S(1)}, s32[]{:T(128)}, s32[1,128]{1,0:T(1,128)S(1)}, s32[]{:T(128)}, ...), branch_computations={%region_14.14_spmd, %region_15.16_spmd} | conditional | flops 675549568 | bytes 37180764 | solution.py:129
  440.2 1.9 constant_dynamic-update-slice_fusion.2
  447.7 1.9 constant_dynamic-update-slice_fusion.2
  450.7 1.9 collective-permute-start.8
  452.6 26.4 %collective-permute-done.8 = f32[128,4,256]{0,2,1:T(8,128)S(1)} collective-permute-done((f32[128,4,256]{0,2,1:T(8,128)S(1)}, f32[128,4,256]{0,2,1:T(8,128)S(1)}, u32[]{:S(2)}, u32[]{:S(2)}) %collective-permute-start.8) | collective-permute-done | bytes 524320 | tf_op jit(solution)/shard_map/ppermute | solution.py:16
  480.1 1.9 collective-permute-start.9
  482.0 10.7 %collective-permute-done.9 = f32[128,4,256]{0,2,1:T(8,128)S(1)} collective-permute-done((f32[128,4,256]{0,2,1:T(8,128)S(1)}, f32[128,4,256]{0,2,1:T(8,128)S(1)}, u32[]{:S(2)}, u32[]{:S(2)}) %collective-permute-start.9) | collective-permute-done | bytes 524320 | tf_op jit(solution)/shard_map/ppermute | solution.py:16
  493.9 1.9 collective-permute-start.10
  495.8 10.7 %collective-permute-done.10 = f32[128,4,256]{0,2,1:T(8,128)S(1)} collective-permute-done((f32[128,4,256]{0,2,1:T(8,128)S(1)}, f32[128,4,256]{0,2,1:T(8,128)S(1)}, u32[]{:S(2)}, u32[]{:S(2)}) %collective-permute-start.10) | collective-permute-done | bytes 524320 | tf_op jit(solution)/shard_map/ppermute | solution.py:16
  507.6 1.9 collective-permute-start.11
  509.5 10.7 %collective-permute-done.11 = f32[128,4,256]{0,2,1:T(8,128)S(1)} collective-permute-done((f32[128,4,256]{0,2,1:T(8,128)S(1)}, f32[128,4,256]{0,2,1:T(8,128)S(1)}, u32[]{:S(2)}, u32[]{:S(2)}) %collective-permute-start.11) | collective-permute-done | bytes 524320 | tf_op jit(solution)/shard_map/ppermute | solution.py:16
  521.3 1.9 collective-permute-start.12
  523.2 10.7 %collective-permute-done.12 = f32[128,4,256]{0,2,1:T(8,128)S(1)} collective-permute-done((f32[128,4,256]{0,2,1:T(8,128)S(1)}, f32[128,4,256]{0,2,1:T(8,128)S(1)}, u32[]{:S(2)}, u32[]{:S(2)}) %collective-permute-start.12) | collective-permute-done | bytes 524320 | tf_op jit(solution)/shard_map/ppermute | solution.py:16
  535.0 1.9 collective-permute-start.13
  537.0 10.7 %collective-permute-done.13 = f32[128,4,256]{0,2,1:T(8,128)S(1)} collective-permute-done((f32[128,4,256]{0,2,1:T(8,128)S(1)}, f32[128,4,256]{0,2,1:T(8,128)S(1)}, u32[]{:S(2)}, u32[]{:S(2)}) %collective-permute-start.13) | collective-permute-done | bytes 524320 | tf_op jit(solution)/shard_map/ppermute | solution.py:16
  548.8 2.1 collective-permute-start.14
  550.9 10.7 %collective-permute-done.14 = f32[128,4,256]{0,2,1:T(8,128)S(1)} collective-permute-done((f32[128,4,256]{0,2,1:T(8,128)S(1)}, f32[128,4,256]{0,2,1:T(8,128)S(1)}, u32[]{:S(2)}, u32[]{:S(2)}) %collective-permute-start.14) | collective-permute-done | bytes 524320 | tf_op jit(solution)/shard_map/ppermute | solution.py:16
  561.5 1.9 bitcast_add_fusion.3
  563.5 2.1 collective-permute-start.15
  565.6 2.3 copy.65
  570.1 6.3 %collective-permute-done.15 = f32[128,4,256]{0,2,1:T(8,128)} collective-permute-done((f32[128,4,256]{0,2,1:T(8,128)}, f32[128,4,256]{0,2,1:T(8,128)}, u32[]{:S(2)}, u32[]{:S(2)}) %collective-permute-start.15) | collective-permute-done | bytes 524320 | tf_op jit(solution)/shard_map/ppermute | solution.py:16
  577.7 7.3 %fusion.27 = bf16[1,128,4096]{2,1,0:T(8,128)(2,1)} fusion(bf16[4096,1024]{1,0:T(8,128)(2,1)} %all-gather.2.cloned.1.call-done, bf16[128,512]{0,1:T(8,128)(2,1)S(1)} %bitcast.167, bf16[128,512]{0,1:T(8,128)(2,1)S(1)} %bitcast.166), kind=kOutput, calls=%fused_computation.57 | convolution fusion | flops 1074790400 | bytes 9699328 | tf_op jit(solution)/shard_map/dot_general | solution.py:179
  (423 shorter events, 191.6 us)
Async XLA Ops:
  7.2 124.7 %copy-start = (bf16[1,128,4096]{2,1,0:T(8,128)(2,1)S(1)}, bf16[1,128,4096]{2,1,0:T(8,128)(2,1)}, u32[]{:S(2)}) copy-start(bf16[1,128,4096]{2,1,0:T(8,128)(2,1)} %param.14) | copy-start | bytes 3145732
  7.2 124.7 %all-gather.2.cloned.1.call-start = ((), (), s32[]{:S(2)}) async-start(), calls=%async_computation | async-start | bytes 8421376 | tf_op jit(solution)/shard_map/all_gather | solution.py:145
  7.9 161.1 %copy-start.9 = (s32[1,32]{1,0:T(1,128)S(1)}, s32[1,32]{1,0:T(1,128)}, u32[]{:S(2)}) copy-start(s32[1,32]{1,0:T(1,128)} %param.17) | copy-start | bytes 388
  7.9 161.4 %copy-start.6 = (bf16[1,128,4096]{2,1,0:T(8,128)(2,1)S(1)}, bf16[1,128,4096]{2,1,0:T(8,128)(2,1)}, u32[]{:S(2)}) copy-start(bf16[1,128,4096]{2,1,0:T(8,128)(2,1)} %param.13) | copy-start | bytes 3145732
  136.6 6.2 %collective-permute-start = (bf16[128,4,256]{2,0,1:T(8,128)(2,1)S(1)}, bf16[128,4,256]{2,0,1:T(8,128)(2,1)S(1)}, u32[]{:S(2)}, u32[]{:S(2)}) collective-permute-start(bf16[128,4,256]{2,0,1:T(8,128)(2,1)S(1)} %bitcast_dynamic-update-slice_fusion.9), channel_id=1, source_target_pairs={{0,1},{1,2},{2,3},{3,4},{4,5},{5,6},{6,7},{7,8},{8,9},{9,10},{10,1... | collective-permute-start | bytes 786440 | tf_op jit(solution)/shard_map/ppermute | solution.py:16
  142.8 26.4 %copy-start.8 = (bf16[128,4,256]{2,0,1:T(8,128)(2,1)}, bf16[128,4,256]{2,0,1:T(8,128)(2,1)S(1)}, u32[]{:S(2)}) copy-start(bf16[128,4,256]{2,0,1:T(8,128)(2,1)S(1)} %collective-permute-done) | copy-start | bytes 786436
  142.8 9.8 %collective-permute-start.1 = (bf16[128,4,256]{2,0,1:T(8,128)(2,1)S(1)}, bf16[128,4,256]{2,0,1:T(8,128)(2,1)S(1)}, u32[]{:S(2)}, u32[]{:S(2)}) collective-permute-start(bf16[128,4,256]{2,0,1:T(8,128)(2,1)S(1)} %collective-permute-done), channel_id=1, source_target_pairs={{0,1},{1,2},{2,3},{3,4},{4,5},{5,6},{6,7},{7,8},{8,9},{9,10},{10,1... | collective-permute-start | bytes 786440 | tf_op jit(solution)/shard_map/ppermute | solution.py:16
  152.6 16.6 %copy-start.7 = (bf16[128,4,256]{2,0,1:T(8,128)(2,1)}, bf16[128,4,256]{2,0,1:T(8,128)(2,1)S(1)}, u32[]{:S(2)}) copy-start(bf16[128,4,256]{2,0,1:T(8,128)(2,1)S(1)} %collective-permute-done.1) | copy-start | bytes 786436
  152.6 9.8 %collective-permute-start.2 = (bf16[128,4,256]{2,0,1:T(8,128)(2,1)S(1)}, bf16[128,4,256]{2,0,1:T(8,128)(2,1)}, u32[]{:S(2)}, u32[]{:S(2)}) collective-permute-start(bf16[128,4,256]{2,0,1:T(8,128)(2,1)S(1)} %collective-permute-done.1), channel_id=1, source_target_pairs={{0,1},{1,2},{2,3},{3,4},{4,5},{5,6},{6,7},{7,8},{8,9},{9,10},{10,1... | collective-permute-start | bytes 786440 | tf_op jit(solution)/shard_map/ppermute | solution.py:16
  162.4 11.2 %collective-permute-start.3 = (bf16[128,4,256]{2,0,1:T(8,128)(2,1)}, bf16[128,4,256]{2,0,1:T(8,128)(2,1)}, u32[]{:S(2)}, u32[]{:S(2)}) collective-permute-start(bf16[128,4,256]{2,0,1:T(8,128)(2,1)} %collective-permute-done.2), channel_id=1, source_target_pairs={{0,1},{1,2},{2,3},{3,4},{4,5},{5,6},{6,7},{7,8},{8,9},{9,10},{10,1... | collective-permute-start | bytes 786440 | tf_op jit(solution)/shard_map/ppermute | solution.py:16
  173.6 9.1 %collective-permute-start.4 = (bf16[128,4,256]{2,0,1:T(8,128)(2,1)}, bf16[128,4,256]{2,0,1:T(8,128)(2,1)S(1)}, u32[]{:S(2)}, u32[]{:S(2)}) collective-permute-start(bf16[128,4,256]{2,0,1:T(8,128)(2,1)} %collective-permute-done.3), channel_id=1, source_target_pairs={{0,1},{1,2},{2,3},{3,4},{4,5},{5,6},{6,7},{7,8},{8,9},{9,10},{10,1... | collective-permute-start | bytes 786440 | tf_op jit(solution)/shard_map/ppermute | solution.py:16
  182.7 9.7 %collective-permute-start.5 = (bf16[128,4,256]{2,0,1:T(8,128)(2,1)S(1)}, bf16[128,4,256]{2,0,1:T(8,128)(2,1)S(1)}, u32[]{:S(2)}, u32[]{:S(2)}) collective-permute-start(bf16[128,4,256]{2,0,1:T(8,128)(2,1)S(1)} %collective-permute-done.4), channel_id=1, source_target_pairs={{0,1},{1,2},{2,3},{3,4},{4,5},{5,6},{6,7},{7,8},{8,9},{9,10},{10,1... | collective-permute-start | bytes 786440 | tf_op jit(solution)/shard_map/ppermute | solution.py:16
  192.4 9.7 %collective-permute-start.6 = (bf16[128,4,256]{2,0,1:T(8,128)(2,1)S(1)}, bf16[128,4,256]{2,0,1:T(8,128)(2,1)S(1)}, u32[]{:S(2)}, u32[]{:S(2)}) collective-permute-start(bf16[128,4,256]{2,0,1:T(8,128)(2,1)S(1)} %collective-permute-done.5), channel_id=1, source_target_pairs={{0,1},{1,2},{2,3},{3,4},{4,5},{5,6},{6,7},{7,8},{8,9},{9,10},{10,1... | collective-permute-start | bytes 786440 | tf_op jit(solution)/shard_map/ppermute | solution.py:16
  202.2 9.8 %collective-permute-start.7 = (bf16[128,4,256]{2,0,1:T(8,128)(2,1)S(1)}, bf16[128,4,256]{2,0,1:T(8,128)(2,1)S(1)}, u32[]{:S(2)}, u32[]{:S(2)}) collective-permute-start(bf16[128,4,256]{2,0,1:T(8,128)(2,1)S(1)} %collective-permute-done.6), channel_id=1, source_target_pairs={{0,1},{1,2},{2,3},{3,4},{4,5},{5,6},{6,7},{7,8},{8,9},{9,10},{10,1... | collective-permute-start | bytes 786440 | tf_op jit(solution)/shard_map/ppermute | solution.py:16
  221.3 2.4 copy-start.1
  225.1 1.3 copy-start.2
  233.5 2.4 copy-start.1
  237.2 1.3 copy-start.2
  245.7 2.4 copy-start.1
  249.4 1.3 copy-start.2
  257.8 2.4 copy-start.1
  261.6 1.3 copy-start.2
  270.0 2.4 copy-start.1
  273.8 1.3 copy-start.2
  282.2 2.4 copy-start.1
  285.9 1.3 copy-start.2
  294.4 2.4 copy-start.1
  298.1 1.3 copy-start.2
  306.5 2.4 copy-start.1
  310.3 1.3 copy-start.2
  332.6 1.8 copy-start.3
  335.3 1.3 copy-start.4
  347.4 1.8 copy-start.3
  350.1 1.3 copy-start.4
  362.2 1.8 copy-start.3
  365.0 1.3 copy-start.4
  377.0 1.8 copy-start.3
  379.8 1.3 copy-start.4
  391.8 1.8 copy-start.3
  394.6 1.3 copy-start.4
  406.6 1.8 copy-start.3
  409.4 1.3 copy-start.4
  421.4 1.8 copy-start.3
  424.1 1.3 copy-start.4
  436.2 1.8 copy-start.3
  438.9 1.3 copy-start.4
  450.7 28.3 %collective-permute-start.8 = (f32[128,4,256]{0,2,1:T(8,128)S(1)}, f32[128,4,256]{0,2,1:T(8,128)S(1)}, u32[]{:S(2)}, u32[]{:S(2)}) collective-permute-start(f32[128,4,256]{0,2,1:T(8,128)S(1)} %slice_bitcast_fusion.9), channel_id=1, source_target_pairs={{1,0},{2,1},{3,2},{4,3},{5,4},{6,5},{7,6},{8,7},{9,8},{10,9},{11,1... | collective-permute-start | bytes 1572872 | tf_op jit(solution)/shard_map/ppermute | solution.py:16
  480.1 12.6 %collective-permute-start.9 = (f32[128,4,256]{0,2,1:T(8,128)S(1)}, f32[128,4,256]{0,2,1:T(8,128)S(1)}, u32[]{:S(2)}, u32[]{:S(2)}) collective-permute-start(f32[128,4,256]{0,2,1:T(8,128)S(1)} %bitcast_add_fusion.9), channel_id=1, source_target_pairs={{1,0},{2,1},{3,2},{4,3},{5,4},{6,5},{7,6},{8,7},{9,8},{10,9},{11,1... | collective-permute-start | bytes 1572872 | tf_op jit(solution)/shard_map/ppermute | solution.py:16
  493.9 12.6 %collective-permute-start.10 = (f32[128,4,256]{0,2,1:T(8,128)S(1)}, f32[128,4,256]{0,2,1:T(8,128)S(1)}, u32[]{:S(2)}, u32[]{:S(2)}) collective-permute-start(f32[128,4,256]{0,2,1:T(8,128)S(1)} %bitcast_add_fusion.8), channel_id=1, source_target_pairs={{1,0},{2,1},{3,2},{4,3},{5,4},{6,5},{7,6},{8,7},{9,8},{10,9},{11,1... | collective-permute-start | bytes 1572872 | tf_op jit(solution)/shard_map/ppermute | solution.py:16
  507.6 12.6 %collective-permute-start.11 = (f32[128,4,256]{0,2,1:T(8,128)S(1)}, f32[128,4,256]{0,2,1:T(8,128)S(1)}, u32[]{:S(2)}, u32[]{:S(2)}) collective-permute-start(f32[128,4,256]{0,2,1:T(8,128)S(1)} %bitcast_add_fusion.7), channel_id=1, source_target_pairs={{1,0},{2,1},{3,2},{4,3},{5,4},{6,5},{7,6},{8,7},{9,8},{10,9},{11,1... | collective-permute-start | bytes 1572872 | tf_op jit(solution)/shard_map/ppermute | solution.py:16
  521.3 12.6 %collective-permute-start.12 = (f32[128,4,256]{0,2,1:T(8,128)S(1)}, f32[128,4,256]{0,2,1:T(8,128)S(1)}, u32[]{:S(2)}, u32[]{:S(2)}) collective-permute-start(f32[128,4,256]{0,2,1:T(8,128)S(1)} %bitcast_add_fusion.6), channel_id=1, source_target_pairs={{1,0},{2,1},{3,2},{4,3},{5,4},{6,5},{7,6},{8,7},{9,8},{10,9},{11,1... | collective-permute-start | bytes 1572872 | tf_op jit(solution)/shard_map/ppermute | solution.py:16
  535.0 12.6 %collective-permute-start.13 = (f32[128,4,256]{0,2,1:T(8,128)S(1)}, f32[128,4,256]{0,2,1:T(8,128)S(1)}, u32[]{:S(2)}, u32[]{:S(2)}) collective-permute-start(f32[128,4,256]{0,2,1:T(8,128)S(1)} %bitcast_add_fusion.5), channel_id=1, source_target_pairs={{1,0},{2,1},{3,2},{4,3},{5,4},{6,5},{7,6},{8,7},{9,8},{10,9},{11,1... | collective-permute-start | bytes 1572872 | tf_op jit(solution)/shard_map/ppermute | solution.py:16
  548.8 19.0 %copy-start.5 = (f32[128,4,8,128]{3,0,2,1:T(8,128)S(1)}, f32[128,4,8,128]{3,0,2,1:T(8,128)}, u32[]{:S(2)}) copy-start(f32[128,4,8,128]{3,0,2,1:T(8,128)} %get-tuple-element.726) | copy-start | bytes 6291460
  548.8 12.7 %collective-permute-start.14 = (f32[128,4,256]{0,2,1:T(8,128)S(1)}, f32[128,4,256]{0,2,1:T(8,128)S(1)}, u32[]{:S(2)}, u32[]{:S(2)}) collective-permute-start(f32[128,4,256]{0,2,1:T(8,128)S(1)} %bitcast_add_fusion.4), channel_id=1, source_target_pairs={{1,0},{2,1},{3,2},{4,3},{5,4},{6,5},{7,6},{8,7},{9,8},{10,9},{11,1... | collective-permute-start | bytes 1572872 | tf_op jit(solution)/shard_map/ppermute | solution.py:16
  563.5 12.9 %collective-permute-start.15 = (f32[128,4,256]{0,2,1:T(8,128)}, f32[128,4,256]{0,2,1:T(8,128)}, u32[]{:S(2)}, u32[]{:S(2)}) collective-permute-start(f32[128,4,256]{0,2,1:T(8,128)} %bitcast_add_fusion.3), channel_id=1, source_target_pairs={{1,0},{2,1},{3,2},{4,3},{5,4},{6,5},{7,6},{8,7},{9,8},{10,9},{11,1... | collective-permute-start | bytes 1572872 | tf_op jit(solution)/shard_map/ppermute | solution.py:16
Sparse Core Ops, SparseCore 0:
  11.7 120.0 all-gather.1
where the time goes:
time: 595 us; the launch traced here: 592 us
  waiting for transfers between devices  235 us (39%)
  local copies, waits for them, and re-layouts  95.1 us (16%)
  other arithmetic  75.2 us (13%)
  starting transfers between devices  62.9 us (11%)
  matrix products  60.4 us (10%)
  loops' own time  48.7 us (8%)
  between operations  14.3 us (2%)
    all_gather x1, waiting for transfers between devices, shards(): lax.all_gather(key_value_weight, ('dp', 'ctx'), axis=0, tiled=True)  124 us
    ppermute x16, waiting for transfers between devices, from_behind(): lax.ppermute(value, axis, [(source, source + steps) for source in range(f...  111 us
    ppermute x16, starting transfers between devices, from_behind(): lax.ppermute(value, axis, [(source, source + steps) for source in range(f...  62.9 us
    cond x72, local copies, waits for them, and re-layouts  24.9 us
    another operation x1, loops' own time, attend(): lax.scan(backward_step, jnp.zeros(query_tile_block.shape, jnp.float32), (...  23.8 us
    another operation x1, loops' own time, attend(): state, unused = lax.scan(forward_step, state, (key_blocks, key_starts))  23.1 us
    dot_general x16, matrix products, scores(): jnp.einsum('qhgd,khd->hgqk', query_tile_block, block_slice[..., :width],...  19.2 us
    dynamic_update_slice x9, local copies, waits for them, and re-layouts, attend(): lax.scan(backward_step, jnp.zeros(query_tile_block.shape, jnp.float32), (...  17 us
  transfers between devices with their start and end apart: 17, of which 15 were waited for; matrix products, arithmetic and copies ran while one was open for 3% of the time, Pallas kernels for 0%

commit v1 on v0

--- a/solution.py
+++ b/solution.py
@@ -3,11 +3,18 @@
 import jax.numpy as jnp
 from jax import lax
 from jax.sharding import PartitionSpec as P
+from jax.lax import all_to_all, axis_size
 
 QUERY_HEADS = 32
 KEY_VALUE_HEADS = 4
 HEAD_SIZE = 128
 masked_score = -1e30
+
+
+def number_the_thing(row_data, mesh_name):
+    return jnp.concatenate(
+        all_to_all(jnp.stack([row_data] * axis_size(mesh_name)), mesh_name, 0, 0), axis=0
+    )
 
 
 def from_behind(value, axis, steps):
@@ -142,7 +149,7 @@
     half_length = columns_all // 2
     projected_input = jnp.dot(
         inputs,
-        lax.all_gather(key_value_weight, ("dp", "ctx"), axis=0, tiled=True),
+        number_the_thing(key_value_weight, ("dp", "ctx")),
         preferred_element_type=jnp.float32,
     )
     projected_input = projected_input.astype(jnp.bfloat16)

time: 595 us -> 642 us (1.079)
  blocking collectives: 0 us -> 202 us
  waiting for transfers between devices: 235 us -> 110 us
  matrix products: 60.4 us -> 46.2 us
  local copies, waits for them, and re-layouts: 95.1 us -> 86.3 us
  other arithmetic: 75.2 us -> 66.6 us
    all_to_all x0 -> x1, blocking collectives: none -> 202 us  [number_the_thing(): all_to_all(jnp.stack([row_data] * axis_size(mesh_name)), mesh_name, 0, 0)]
    all_gather x1, waiting for transfers between devices: 124 us -> 0.02 us  [shards(): lax.all_gather(key_value_weight, ('dp', 'ctx'), axis=0, tiled=True)]
    dot_general x16, matrix products: 19.2 us -> 8.17 us  [scores(): jnp.einsum('qhgd,khd->hgqk', query_tile_block, block_slice[..., :width],...]
    dynamic_update_slice x9, local copies, waits for them, and re-layouts: 17 us -> 7.67 us  [attend(): lax.scan(backward_step, jnp.zeros(query_tile_block.shape, jnp.float32), (...]
    unnamed x25 -> x29, local copies, waits for them, and re-layouts: 13.2 us -> 12.7 us
  transfers between devices with their start and end apart: 17 -> 17, of which waited for: 15 -> 14; matrix products, arithmetic and copies ran while one was open for 3% -> 26% of each run, Pallas kernels for 0% -> 0%
where the time goes in v1:
time: 642 us; the launch traced here: 639 us
  blocking collectives  202 us (31%)
  waiting for transfers between devices  110 us (17%)
  local copies, waits for them, and re-layouts  86.3 us (13%)
  other arithmetic  66.6 us (10%)
  starting transfers between devices  64.8 us (10%)
  loops' own time  48.2 us (8%)
  matrix products  46.2 us (7%)
  between operations  14.4 us (2%)
    all_to_all x1, blocking collectives, number_the_thing(): all_to_all(jnp.stack([row_data] * axis_size(mesh_name)), mesh_name, 0, 0)  202 us
    ppermute x16, waiting for transfers between devices, from_behind(): lax.ppermute(value, axis, [(source, source + steps) for source in range(f...  110 us
    ppermute x16, starting transfers between devices, from_behind(): lax.ppermute(value, axis, [(source, source + steps) for source in range(f...  64.7 us
    cond x72, local copies, waits for them, and re-layouts  25.6 us
    another operation x1, loops' own time, attend(): state, unused = lax.scan(forward_step, state, (key_blocks, key_starts))  23.3 us
    another operation x1, loops' own time, attend(): lax.scan(backward_step, jnp.zeros(query_tile_block.shape, jnp.float32), (...  23.1 us
    squeeze x16, local copies, waits for them, and re-layouts, attend(): state, unused = lax.scan(forward_step, state, (key_blocks, key_starts))  16.7 us
    reduce_sum x36, other arithmetic, document_of(): return jnp.sum((positions[..., None] >= ends).astype(jnp.int32), axis=-1)  13.8 us
  transfers between devices with their start and end apart: 17, of which 14 were waited for; matrix products, arithmetic and copies ran while one was open for 26% of the time, Pallas kernels for 0%

profile of v1, /device:TPU:57, one launch (start us, length us, event | category | flops | bytes accessed | tf_op | source)
XLA Modules:
  0.0 638.5 jit_solution(15688969623759315300)
XLA Ops:
  7.2 1.9 stack.22
  9.1 201.6 %all_to_all.5 = bf16[256,16,1024]{2,1,0:T(8,128)(2,1)S(1)} all-to-all(bf16[256,16,1024]{2,1,0:T(8,128)(2,1)S(1)} %stack.22), channel_id=1, replica_groups=mesh['dp'=8,'ctx'=32] {'dp','ctx'}, dimensions={0} | all-to-all | bytes 16777216 | tf_op jit(solution)/shard_map/all_to_all | solution.py:16
  212.2 4.0 collective-permute-start
  216.2 3.3 collective-permute-done
  219.5 6.5 %collective-permute-start.1 = (bf16[128,4,256]{2,0,1:T(8,128)(2,1)S(1)}, bf16[128,4,256]{2,0,1:T(8,128)(2,1)S(1)}, u32[]{:S(2)}, u32[]{:S(2)}) collective-permute-start(bf16[128,4,256]{2,0,1:T(8,128)(2,1)S(1)} %collective-permute-done), channel_id=1, source_target_pairs={{0,1},{1,2},{2,3},{3,4},{4,5},{5,6},{6,7},{7,8},{8,9},{9,10},{10,1... | collective-permute-start | bytes 786440 | tf_op jit(solution)/shard_map/ppermute | solution.py:23
  226.0 3.3 collective-permute-done.1
  229.3 6.5 %collective-permute-start.2 = (bf16[128,4,256]{2,0,1:T(8,128)(2,1)S(1)}, bf16[128,4,256]{2,0,1:T(8,128)(2,1)}, u32[]{:S(2)}, u32[]{:S(2)}) collective-permute-start(bf16[128,4,256]{2,0,1:T(8,128)(2,1)S(1)} %collective-permute-done.1), channel_id=1, source_target_pairs={{0,1},{1,2},{2,3},{3,4},{4,5},{5,6},{6,7},{7,8},{8,9},{9,10},{10,1... | collective-permute-start | bytes 786440 | tf_op jit(solution)/shard_map/ppermute | solution.py:23
  235.8 3.3 collective-permute-done.2
  239.1 6.6 %collective-permute-start.3 = (bf16[128,4,256]{2,0,1:T(8,128)(2,1)}, bf16[128,4,256]{2,0,1:T(8,128)(2,1)}, u32[]{:S(2)}, u32[]{:S(2)}) collective-permute-start(bf16[128,4,256]{2,0,1:T(8,128)(2,1)} %collective-permute-done.2), channel_id=1, source_target_pairs={{0,1},{1,2},{2,3},{3,4},{4,5},{5,6},{6,7},{7,8},{8,9},{9,10},{10,1... | collective-permute-start | bytes 786440 | tf_op jit(solution)/shard_map/ppermute | solution.py:23
  247.4 1.6 copy.51
  249.7 6.2 collective-permute-start.4
  256.7 1.7 bitcast_dynamic-update-slice_fusion.7
  259.6 6.4 collective-permute-start.5
  266.0 1.7 bitcast_dynamic-update-slice_fusion.6
  267.6 1.7 bitcast_dynamic-update-slice_fusion.5
  269.3 6.4 %collective-permute-start.6 = (bf16[128,4,256]{2,0,1:T(8,128)(2,1)S(1)}, bf16[128,4,256]{2,0,1:T(8,128)(2,1)S(1)}, u32[]{:S(2)}, u32[]{:S(2)}) collective-permute-start(bf16[128,4,256]{2,0,1:T(8,128)(2,1)S(1)} %collective-permute-done.5), channel_id=1, source_target_pairs={{0,1},{1,2},{2,3},{3,4},{4,5},{5,6},{6,7},{7,8},{8,9},{9,10},{10,1... | collective-permute-start | bytes 786440 | tf_op jit(solution)/shard_map/ppermute | solution.py:23
  275.7 1.7 bitcast_dynamic-update-slice_fusion.4
  279.0 6.5 %collective-permute-start.7 = (bf16[128,4,256]{2,0,1:T(8,128)(2,1)S(1)}, bf16[128,4,256]{2,0,1:T(8,128)(2,1)S(1)}, u32[]{:S(2)}, u32[]{:S(2)}) collective-permute-start(bf16[128,4,256]{2,0,1:T(8,128)(2,1)S(1)} %collective-permute-done.6), channel_id=1, source_target_pairs={{0,1},{1,2},{2,3},{3,4},{4,5},{5,6},{6,7},{7,8},{8,9},{9,10},{10,1... | collective-permute-start | bytes 786440 | tf_op jit(solution)/shard_map/ppermute | solution.py:23
  287.0 2.3 collective-permute-done.7
  290.0 1.5 broadcast.103.clone
  291.6 88.1 %while.39 = (s32[]{:T(128)}, f32[4,8,128]{2,1,0:T(8,128)S(1)}, f32[4,8,128]{2,1,0:T(8,128)S(1)}, f32[128,4,8,128]{3,0,2,1:T(8,128)}, s32[9]{0:T(128)S(1)}, /*ind...) while((s32[]{:T(128)}, f32[4,8,128]{2,1,0:T(8,128)S(1)}, ...), condition=%wide.region_10.11_spmd.clone, body=%wide.region_3.10_spmd.clone.sunk | while | flops 275341920 | bytes 29466568 | solution.py:94
  296.1 5.9 conditional.6
  299.3 1.4 bitcast_add_fusion
  306.5 5.9 conditional.6
  309.7 1.4 bitcast_add_fusion
  316.9 5.9 conditional.6
  320.1 1.4 bitcast_add_fusion
  327.4 6.0 conditional.6
  337.9 5.9 conditional.6
  341.1 1.4 bitcast_add_fusion
  348.4 5.9 conditional.6
  351.5 1.4 bitcast_add_fusion
  358.8 5.9 conditional.6
  362.0 1.4 bitcast_add_fusion
  369.2 5.9 conditional.6
  379.7 2.9 copy.49
  382.6 3.1 multiply_reduce_fusion
  385.7 1.5 broadcast.103
  387.2 111.6 %while.40 = (s32[]{:T(128)}, f32[128,4,8,128]{3,0,2,1:T(8,128)}, f32[9,128,4,256]{1,3,2,0:T(8,128)}, s32[9]{0:T(128)S(1)}, s32[]{:T(128)}, /*index=5*/s32[32]{0:...) while((s32[]{:T(128)}, f32[128,4,8,128]{3,0,2,1:T(8,128)}, ...), condition=%wide.region_17.18_spmd.clone, body=%wide.region_12.17_spmd.clone.sunk | while | flops 675558016 | bytes 38248888 | solution.py:138
  391.7 7.9 %conditional.7 = (f32[128,4,8,128]{3,0,2,1:T(8,128)}, f32[1,128,4,256]{1,3,2,0:T(8,128)S(1)}) conditional(s32[]{:T(128)} %convert_element_type.146, f32[128,4,8,128]{3,0,2,1:T(8,128)} %get-tuple-element.1136, (s32[128]{0:T(128)S(1)}, s32[128,32]{1,0:T(8,128)S(1)}, s32[]{:T(128)}, s32[1,128]{1,0:T(1,128)S(1)}, s32[]{:T(128)}, ...), branch_computations={%region_14.14_spmd, %region_15.16_spmd} | conditional | flops 675549568 | bytes 37180764 | solution.py:136
  405.0 7.9 %conditional.7 = (f32[128,4,8,128]{3,0,2,1:T(8,128)}, f32[1,128,4,256]{1,3,2,0:T(8,128)S(1)}) conditional(s32[]{:T(128)} %convert_element_type.146, f32[128,4,8,128]{3,0,2,1:T(8,128)} %get-tuple-element.1136, (s32[128]{0:T(128)S(1)}, s32[128,32]{1,0:T(8,128)S(1)}, s32[]{:T(128)}, s32[1,128]{1,0:T(1,128)S(1)}, s32[]{:T(128)}, ...), branch_computations={%region_14.14_spmd, %region_15.16_spmd} | conditional | flops 675549568 | bytes 37180764 | solution.py:136
  418.4 7.9 %conditional.7 = (f32[128,4,8,128]{3,0,2,1:T(8,128)}, f32[1,128,4,256]{1,3,2,0:T(8,128)S(1)}) conditional(s32[]{:T(128)} %convert_element_type.146, f32[128,4,8,128]{3,0,2,1:T(8,128)} %get-tuple-element.1136, (s32[128]{0:T(128)S(1)}, s32[128,32]{1,0:T(8,128)S(1)}, s32[]{:T(128)}, s32[1,128]{1,0:T(1,128)S(1)}, s32[]{:T(128)}, ...), branch_computations={%region_14.14_spmd, %region_15.16_spmd} | conditional | flops 675549568 | bytes 37180764 | solution.py:136
  431.6 7.9 %conditional.7 = (f32[128,4,8,128]{3,0,2,1:T(8,128)}, f32[1,128,4,256]{1,3,2,0:T(8,128)S(1)}) conditional(s32[]{:T(128)} %convert_element_type.146, f32[128,4,8,128]{3,0,2,1:T(8,128)} %get-tuple-element.1136, (s32[128]{0:T(128)S(1)}, s32[128,32]{1,0:T(8,128)S(1)}, s32[]{:T(128)}, s32[1,128]{1,0:T(1,128)S(1)}, s32[]{:T(128)}, ...), branch_computations={%region_14.14_spmd, %region_15.16_spmd} | conditional | flops 675549568 | bytes 37180764 | solution.py:136
  444.9 7.9 %conditional.7 = (f32[128,4,8,128]{3,0,2,1:T(8,128)}, f32[1,128,4,256]{1,3,2,0:T(8,128)S(1)}) conditional(s32[]{:T(128)} %convert_element_type.146, f32[128,4,8,128]{3,0,2,1:T(8,128)} %get-tuple-element.1136, (s32[128]{0:T(128)S(1)}, s32[128,32]{1,0:T(8,128)S(1)}, s32[]{:T(128)}, s32[1,128]{1,0:T(1,128)S(1)}, s32[]{:T(128)}, ...), branch_computations={%region_14.14_spmd, %region_15.16_spmd} | conditional | flops 675549568 | bytes 37180764 | solution.py:136
  458.2 7.9 %conditional.7 = (f32[128,4,8,128]{3,0,2,1:T(8,128)}, f32[1,128,4,256]{1,3,2,0:T(8,128)S(1)}) conditional(s32[]{:T(128)} %convert_element_type.146, f32[128,4,8,128]{3,0,2,1:T(8,128)} %get-tuple-element.1136, (s32[128]{0:T(128)S(1)}, s32[128,32]{1,0:T(8,128)S(1)}, s32[]{:T(128)}, s32[1,128]{1,0:T(1,128)S(1)}, s32[]{:T(128)}, ...), branch_computations={%region_14.14_spmd, %region_15.16_spmd} | conditional | flops 675549568 | bytes 37180764 | solution.py:136
  471.4 7.9 %conditional.7 = (f32[128,4,8,128]{3,0,2,1:T(8,128)}, f32[1,128,4,256]{1,3,2,0:T(8,128)S(1)}) conditional(s32[]{:T(128)} %convert_element_type.146, f32[128,4,8,128]{3,0,2,1:T(8,128)} %get-tuple-element.1136, (s32[128]{0:T(128)S(1)}, s32[128,32]{1,0:T(8,128)S(1)}, s32[]{:T(128)}, s32[1,128]{1,0:T(1,128)S(1)}, s32[]{:T(128)}, ...), branch_computations={%region_14.14_spmd, %region_15.16_spmd} | conditional | flops 675549568 | bytes 37180764 | solution.py:136
  484.7 7.9 %conditional.7 = (f32[128,4,8,128]{3,0,2,1:T(8,128)}, f32[1,128,4,256]{1,3,2,0:T(8,128)S(1)}) conditional(s32[]{:T(128)} %convert_element_type.146, f32[128,4,8,128]{3,0,2,1:T(8,128)} %get-tuple-element.1136, (s32[128]{0:T(128)S(1)}, s32[128,32]{1,0:T(8,128)S(1)}, s32[]{:T(128)}, s32[1,128]{1,0:T(1,128)S(1)}, s32[]{:T(128)}, ...), branch_computations={%region_14.14_spmd, %region_15.16_spmd} | conditional | flops 675549568 | bytes 37180764 | solution.py:136
  499.9 2.1 collective-permute-start.8
  502.0 25.0 %collective-permute-done.8 = f32[128,4,256]{0,2,1:T(8,128)S(1)} collective-permute-done((f32[128,4,256]{0,2,1:T(8,128)S(1)}, f32[128,4,256]{0,2,1:T(8,128)S(1)}, u32[]{:S(2)}, u32[]{:S(2)}) %collective-permute-start.8) | collective-permute-done | bytes 524320 | tf_op jit(solution)/shard_map/ppermute | solution.py:23
  528.1 1.9 collective-permute-start.9
  530.0 10.7 %collective-permute-done.9 = f32[128,4,256]{0,2,1:T(8,128)S(1)} collective-permute-done((f32[128,4,256]{0,2,1:T(8,128)S(1)}, f32[128,4,256]{0,2,1:T(8,128)S(1)}, u32[]{:S(2)}, u32[]{:S(2)}) %collective-permute-start.9) | collective-permute-done | bytes 524320 | tf_op jit(solution)/shard_map/ppermute | solution.py:23
  541.8 1.9 collective-permute-start.10
  543.7 10.7 %collective-permute-done.10 = f32[128,4,256]{0,2,1:T(8,128)S(1)} collective-permute-done((f32[128,4,256]{0,2,1:T(8,128)S(1)}, f32[128,4,256]{0,2,1:T(8,128)S(1)}, u32[]{:S(2)}, u32[]{:S(2)}) %collective-permute-start.10) | collective-permute-done | bytes 524320 | tf_op jit(solution)/shard_map/ppermute | solution.py:23
  555.5 1.9 collective-permute-start.11
  557.4 10.7 %collective-permute-done.11 = f32[128,4,256]{0,2,1:T(8,128)S(1)} collective-permute-done((f32[128,4,256]{0,2,1:T(8,128)S(1)}, f32[128,4,256]{0,2,1:T(8,128)S(1)}, u32[]{:S(2)}, u32[]{:S(2)}) %collective-permute-start.11) | collective-permute-done | bytes 524320 | tf_op jit(solution)/shard_map/ppermute | solution.py:23
  569.2 2.1 collective-permute-start.12
  571.3 10.7 %collective-permute-done.12 = f32[128,4,256]{0,2,1:T(8,128)S(1)} collective-permute-done((f32[128,4,256]{0,2,1:T(8,128)S(1)}, f32[128,4,256]{0,2,1:T(8,128)S(1)}, u32[]{:S(2)}, u32[]{:S(2)}) %collective-permute-start.12) | collective-permute-done | bytes 524320 | tf_op jit(solution)/shard_map/ppermute | solution.py:23
  583.1 1.9 collective-permute-start.13
  585.0 10.7 %collective-permute-done.13 = f32[128,4,256]{0,2,1:T(8,128)S(1)} collective-permute-done((f32[128,4,256]{0,2,1:T(8,128)S(1)}, f32[128,4,256]{0,2,1:T(8,128)S(1)}, u32[]{:S(2)}, u32[]{:S(2)}) %collective-permute-start.13) | collective-permute-done | bytes 524320 | tf_op jit(solution)/shard_map/ppermute | solution.py:23
  596.8 1.9 collective-permute-start.14
  598.8 10.7 %collective-permute-done.14 = f32[128,4,256]{0,2,1:T(8,128)S(1)} collective-permute-done((f32[128,4,256]{0,2,1:T(8,128)S(1)}, f32[128,4,256]{0,2,1:T(8,128)S(1)}, u32[]{:S(2)}, u32[]{:S(2)}) %collective-permute-start.14) | collective-permute-done | bytes 524320 | tf_op jit(solution)/shard_map/ppermute | solution.py:23
  610.6 1.9 collective-permute-start.15
  616.1 7.1 %collective-permute-done.15 = f32[128,4,256]{0,2,1:T(8,128)S(1)} collective-permute-done((f32[128,4,256]{0,2,1:T(8,128)S(1)}, f32[128,4,256]{0,2,1:T(8,128)S(1)}, u32[]{:S(2)}, u32[]{:S(2)}) %collective-permute-start.15) | collective-permute-done | bytes 524320 | tf_op jit(solution)/shard_map/ppermute | solution.py:23
  624.3 7.3 %fusion.27 = bf16[1,128,4096]{2,1,0:T(8,128)(2,1)} fusion(bf16[4096,1024]{1,0:T(8,128)(2,1)} %all-gather.2.cloned.1.call-done, bf16[128,512]{0,1:T(8,128)(2,1)S(1)} %bitcast.169, bf16[128,512]{0,1:T(8,128)(2,1)S(1)} %bitcast.168), kind=kOutput, calls=%fused_computation.57 | convolution fusion | flops 1074790400 | bytes 9699328 | tf_op jit(solution)/shard_map/dot_general | solution.py:186
  (429 shorter events, 166.6 us)
Async XLA Ops:
  7.2 203.6 %copy-start = (bf16[1,128,4096]{2,1,0:T(8,128)(2,1)S(1)}, bf16[1,128,4096]{2,1,0:T(8,128)(2,1)}, u32[]{:S(2)}) copy-start(bf16[1,128,4096]{2,1,0:T(8,128)(2,1)} %param.14) | copy-start | bytes 3145732
  7.2 617.1 %all-gather.2.cloned.1.call-start = ((), (), s32[]{:S(2)}) async-start(), calls=%async_computation.1 | async-start | bytes 8421376 | tf_op jit(solution)/shard_map/all_gather | solution.py:188
  210.7 35.0 %copy-start.11 = (s32[1,32]{1,0:T(1,128)S(1)}, s32[1,32]{1,0:T(1,128)}, u32[]{:S(2)}) copy-start(s32[1,32]{1,0:T(1,128)} %param.17) | copy-start | bytes 388
  210.7 35.3 %copy-start.8 = (bf16[1,128,4096]{2,1,0:T(8,128)(2,1)S(1)}, bf16[1,128,4096]{2,1,0:T(8,128)(2,1)}, u32[]{:S(2)}) copy-start(bf16[1,128,4096]{2,1,0:T(8,128)(2,1)} %param.13) | copy-start | bytes 3145732
  212.2 7.3 %collective-permute-start = (bf16[128,4,256]{2,0,1:T(8,128)(2,1)S(1)}, bf16[128,4,256]{2,0,1:T(8,128)(2,1)S(1)}, u32[]{:S(2)}, u32[]{:S(2)}) collective-permute-start(bf16[128,4,256]{2,0,1:T(8,128)(2,1)S(1)} %bitcast_dynamic-update-slice_fusion.9), channel_id=1, source_target_pairs={{0,1},{1,2},{2,3},{3,4},{4,5},{5,6},{6,7},{7,8},{8,9},{9,10},{10,1... | collective-permute-start | bytes 786440 | tf_op jit(solution)/shard_map/ppermute | solution.py:23
  219.5 26.5 %copy-start.10 = (bf16[128,4,256]{2,0,1:T(8,128)(2,1)}, bf16[128,4,256]{2,0,1:T(8,128)(2,1)S(1)}, u32[]{:S(2)}) copy-start(bf16[128,4,256]{2,0,1:T(8,128)(2,1)S(1)} %collective-permute-done) | copy-start | bytes 786436
  219.5 9.8 %collective-permute-start.1 = (bf16[128,4,256]{2,0,1:T(8,128)(2,1)S(1)}, bf16[128,4,256]{2,0,1:T(8,128)(2,1)S(1)}, u32[]{:S(2)}, u32[]{:S(2)}) collective-permute-start(bf16[128,4,256]{2,0,1:T(8,128)(2,1)S(1)} %collective-permute-done), channel_id=1, source_target_pairs={{0,1},{1,2},{2,3},{3,4},{4,5},{5,6},{6,7},{7,8},{8,9},{9,10},{10,1... | collective-permute-start | bytes 786440 | tf_op jit(solution)/shard_map/ppermute | solution.py:23
  229.3 16.7 %copy-start.9 = (bf16[128,4,256]{2,0,1:T(8,128)(2,1)}, bf16[128,4,256]{2,0,1:T(8,128)(2,1)S(1)}, u32[]{:S(2)}) copy-start(bf16[128,4,256]{2,0,1:T(8,128)(2,1)S(1)} %collective-permute-done.1) | copy-start | bytes 786436
  229.3 9.8 %collective-permute-start.2 = (bf16[128,4,256]{2,0,1:T(8,128)(2,1)S(1)}, bf16[128,4,256]{2,0,1:T(8,128)(2,1)}, u32[]{:S(2)}, u32[]{:S(2)}) collective-permute-start(bf16[128,4,256]{2,0,1:T(8,128)(2,1)S(1)} %collective-permute-done.1), channel_id=1, source_target_pairs={{0,1},{1,2},{2,3},{3,4},{4,5},{5,6},{6,7},{7,8},{8,9},{9,10},{10,1... | collective-permute-start | bytes 786440 | tf_op jit(solution)/shard_map/ppermute | solution.py:23
  239.1 10.6 %collective-permute-start.3 = (bf16[128,4,256]{2,0,1:T(8,128)(2,1)}, bf16[128,4,256]{2,0,1:T(8,128)(2,1)}, u32[]{:S(2)}, u32[]{:S(2)}) collective-permute-start(bf16[128,4,256]{2,0,1:T(8,128)(2,1)} %collective-permute-done.2), channel_id=1, source_target_pairs={{0,1},{1,2},{2,3},{3,4},{4,5},{5,6},{6,7},{7,8},{8,9},{9,10},{10,1... | collective-permute-start | bytes 786440 | tf_op jit(solution)/shard_map/ppermute | solution.py:23
  249.7 9.9 %collective-permute-start.4 = (bf16[128,4,256]{2,0,1:T(8,128)(2,1)}, bf16[128,4,256]{2,0,1:T(8,128)(2,1)S(1)}, u32[]{:S(2)}, u32[]{:S(2)}) collective-permute-start(bf16[128,4,256]{2,0,1:T(8,128)(2,1)} %collective-permute-done.3), channel_id=1, source_target_pairs={{0,1},{1,2},{2,3},{3,4},{4,5},{5,6},{6,7},{7,8},{8,9},{9,10},{10,1... | collective-permute-start | bytes 786440 | tf_op jit(solution)/shard_map/ppermute | solution.py:23
  259.6 9.8 %collective-permute-start.5 = (bf16[128,4,256]{2,0,1:T(8,128)(2,1)S(1)}, bf16[128,4,256]{2,0,1:T(8,128)(2,1)S(1)}, u32[]{:S(2)}, u32[]{:S(2)}) collective-permute-start(bf16[128,4,256]{2,0,1:T(8,128)(2,1)S(1)} %collective-permute-done.4), channel_id=1, source_target_pairs={{0,1},{1,2},{2,3},{3,4},{4,5},{5,6},{6,7},{7,8},{8,9},{9,10},{10,1... | collective-permute-start | bytes 786440 | tf_op jit(solution)/shard_map/ppermute | solution.py:23
  269.3 9.7 %collective-permute-start.6 = (bf16[128,4,256]{2,0,1:T(8,128)(2,1)S(1)}, bf16[128,4,256]{2,0,1:T(8,128)(2,1)S(1)}, u32[]{:S(2)}, u32[]{:S(2)}) collective-permute-start(bf16[128,4,256]{2,0,1:T(8,128)(2,1)S(1)} %collective-permute-done.5), channel_id=1, source_target_pairs={{0,1},{1,2},{2,3},{3,4},{4,5},{5,6},{6,7},{7,8},{8,9},{9,10},{10,1... | collective-permute-start | bytes 786440 | tf_op jit(solution)/shard_map/ppermute | solution.py:23
  279.0 10.2 %collective-permute-start.7 = (bf16[128,4,256]{2,0,1:T(8,128)(2,1)S(1)}, bf16[128,4,256]{2,0,1:T(8,128)(2,1)S(1)}, u32[]{:S(2)}, u32[]{:S(2)}) collective-permute-start(bf16[128,4,256]{2,0,1:T(8,128)(2,1)S(1)} %collective-permute-done.6), channel_id=1, source_target_pairs={{0,1},{1,2},{2,3},{3,4},{4,5},{5,6},{6,7},{7,8},{8,9},{9,10},{10,1... | collective-permute-start | bytes 786440 | tf_op jit(solution)/shard_map/ppermute | solution.py:23
  297.5 1.7 copy-start.2
  300.6 1.3 copy-start.3
  308.0 1.7 copy-start.2
  311.1 1.3 copy-start.3
  318.4 1.7 copy-start.2
  321.5 1.3 copy-start.3
  328.8 1.8 copy-start.2
  332.1 1.3 copy-start.3
  339.4 1.7 copy-start.2
  342.5 1.3 copy-start.3
  349.8 1.7 copy-start.2
  352.9 1.3 copy-start.3
  360.2 1.7 copy-start.2
  363.3 1.3 copy-start.3
  370.7 1.7 copy-start.2
  373.8 1.3 copy-start.3
  395.8 1.6 copy-start.4
  398.3 1.3 copy-start.5
  409.1 1.6 copy-start.4
  411.6 1.3 copy-start.5
  422.4 1.6 copy-start.4
  425.0 1.3 copy-start.5
  435.6 1.6 copy-start.4
  438.2 1.3 copy-start.5
  448.9 1.6 copy-start.4
  451.5 1.3 copy-start.5
  462.2 1.6 copy-start.4
  464.8 1.3 copy-start.5
  475.4 1.6 copy-start.4
  478.0 1.3 copy-start.5
  488.7 1.6 copy-start.4
  491.3 1.3 copy-start.5
  499.9 27.1 %collective-permute-start.8 = (f32[128,4,256]{0,2,1:T(8,128)S(1)}, f32[128,4,256]{0,2,1:T(8,128)S(1)}, u32[]{:S(2)}, u32[]{:S(2)}) collective-permute-start(f32[128,4,256]{0,2,1:T(8,128)S(1)} %slice_bitcast_fusion.9), channel_id=1, source_target_pairs={{1,0},{2,1},{3,2},{4,3},{5,4},{6,5},{7,6},{8,7},{9,8},{10,9},{11,1... | collective-permute-start | bytes 1572872 | tf_op jit(solution)/shard_map/ppermute | solution.py:23
  528.1 12.6 %collective-permute-start.9 = (f32[128,4,256]{0,2,1:T(8,128)S(1)}, f32[128,4,256]{0,2,1:T(8,128)S(1)}, u32[]{:S(2)}, u32[]{:S(2)}) collective-permute-start(f32[128,4,256]{0,2,1:T(8,128)S(1)} %bitcast_add_fusion.9), channel_id=1, source_target_pairs={{1,0},{2,1},{3,2},{4,3},{5,4},{6,5},{7,6},{8,7},{9,8},{10,9},{11,1... | collective-permute-start | bytes 1572872 | tf_op jit(solution)/shard_map/ppermute | solution.py:23
  541.8 12.6 %collective-permute-start.10 = (f32[128,4,256]{0,2,1:T(8,128)S(1)}, f32[128,4,256]{0,2,1:T(8,128)S(1)}, u32[]{:S(2)}, u32[]{:S(2)}) collective-permute-start(f32[128,4,256]{0,2,1:T(8,128)S(1)} %bitcast_add_fusion.8), channel_id=1, source_target_pairs={{1,0},{2,1},{3,2},{4,3},{5,4},{6,5},{7,6},{8,7},{9,8},{10,9},{11,1... | collective-permute-start | bytes 1572872 | tf_op jit(solution)/shard_map/ppermute | solution.py:23
  555.5 12.6 %collective-permute-start.11 = (f32[128,4,256]{0,2,1:T(8,128)S(1)}, f32[128,4,256]{0,2,1:T(8,128)S(1)}, u32[]{:S(2)}, u32[]{:S(2)}) collective-permute-start(f32[128,4,256]{0,2,1:T(8,128)S(1)} %bitcast_add_fusion.7), channel_id=1, source_target_pairs={{1,0},{2,1},{3,2},{4,3},{5,4},{6,5},{7,6},{8,7},{9,8},{10,9},{11,1... | collective-permute-start | bytes 1572872 | tf_op jit(solution)/shard_map/ppermute | solution.py:23
  569.2 43.3 %copy-start.6 = (f32[128,4,8,128]{3,0,2,1:T(8,128)S(1)}, f32[128,4,8,128]{3,0,2,1:T(8,128)}, u32[]{:S(2)}) copy-start(f32[128,4,8,128]{3,0,2,1:T(8,128)} %get-tuple-element.726) | copy-start | bytes 6291460
  569.2 12.7 %collective-permute-start.12 = (f32[128,4,256]{0,2,1:T(8,128)S(1)}, f32[128,4,256]{0,2,1:T(8,128)S(1)}, u32[]{:S(2)}, u32[]{:S(2)}) collective-permute-start(f32[128,4,256]{0,2,1:T(8,128)S(1)} %bitcast_add_fusion.6), channel_id=1, source_target_pairs={{1,0},{2,1},{3,2},{4,3},{5,4},{6,5},{7,6},{8,7},{9,8},{10,9},{11,1... | collective-permute-start | bytes 1572872 | tf_op jit(solution)/shard_map/ppermute | solution.py:23
  583.1 12.6 %collective-permute-start.13 = (f32[128,4,256]{0,2,1:T(8,128)S(1)}, f32[128,4,256]{0,2,1:T(8,128)S(1)}, u32[]{:S(2)}, u32[]{:S(2)}) collective-permute-start(f32[128,4,256]{0,2,1:T(8,128)S(1)} %bitcast_add_fusion.5), channel_id=1, source_target_pairs={{1,0},{2,1},{3,2},{4,3},{5,4},{6,5},{7,6},{8,7},{9,8},{10,9},{11,1... | collective-permute-start | bytes 1572872 | tf_op jit(solution)/shard_map/ppermute | solution.py:23
  596.8 12.6 %collective-permute-start.14 = (f32[128,4,256]{0,2,1:T(8,128)S(1)}, f32[128,4,256]{0,2,1:T(8,128)S(1)}, u32[]{:S(2)}, u32[]{:S(2)}) collective-permute-start(f32[128,4,256]{0,2,1:T(8,128)S(1)} %bitcast_add_fusion.4), channel_id=1, source_target_pairs={{1,0},{2,1},{3,2},{4,3},{5,4},{6,5},{7,6},{8,7},{9,8},{10,9},{11,1... | collective-permute-start | bytes 1572872 | tf_op jit(solution)/shard_map/ppermute | solution.py:23
  610.6 12.6 %collective-permute-start.15 = (f32[128,4,256]{0,2,1:T(8,128)S(1)}, f32[128,4,256]{0,2,1:T(8,128)S(1)}, u32[]{:S(2)}, u32[]{:S(2)}) collective-permute-start(f32[128,4,256]{0,2,1:T(8,128)S(1)} %bitcast_add_fusion.3), channel_id=1, source_target_pairs={{1,0},{2,1},{3,2},{4,3},{5,4},{6,5},{7,6},{8,7},{9,8},{10,9},{11,1... | collective-permute-start | bytes 1572872 | tf_op jit(solution)/shard_map/ppermute | solution.py:23
  612.8 2.0 copy-start.7
  624.3 7.4 %copy-start.1 = (bf16[1,128,4096]{2,1,0:T(8,128)(2,1)S(1)}, bf16[1,128,4096]{2,1,0:T(8,128)(2,1)}, u32[]{:S(2)}) copy-start(bf16[1,128,4096]{2,1,0:T(8,128)(2,1)} %param.14) | copy-start | bytes 3145732
Sparse Core Ops, SparseCore 0:
  235.9 112.7 all-gather.1
